TPU v7x, 256 devices: a whole 4x4x8 slice. The times are simulated.
256 devices in a mesh: pb: 64 (over z, y_hi, x), br: 4 (over y_lo, core).
Axes of the slice: x: 4, y: 4 (y_hi: 2, y_lo: 2; y = y_hi * 2 + y_lo), z: 8, core: 2. Of those that a mesh axis runs over, the one named last changes fastest.
Arguments:
- bloch_const: bfloat16 [36, 663552], P(None, 'pb'), may hold values from -1 to 1
- polarization: bfloat16 [36, 512, 36], P('br', 'pb'), may hold values from -1 to 1
- delta_weight: bfloat16 [36, 512, 18432], P('br', None, 'pb'), may hold values from 0.02 to 3
- partner: int32 [512, 512], P('pb'), may hold values from 0 to 511, each once within a row
- velocity: float32 [512, 36], P('pb', 'br'), may hold values from -0.5 to 1.5
- capacity: float32 [512, 36], P('pb', 'br'), may hold values from 0.2 to 2
Outputs:
- deviation: float32 [512, 36], P('pb', 'br')
- kappa: float32 [2], replicated
Inputs may be any that keep to these rules, and one draw needn't show every extreme that they name: For each q, partner[q, :] names every q-point exactly once.
All inputs are finite; a program needn't handle non-finite values.
Results may differ from a plain program's by a relative error of at most 0.0003.
Values may be sent and summed in bfloat16 or wider, within the bound.
A program may use at most 192 MiB of HBM per device.

v0:
```python
from functools import partial
import jax
import jax.numpy as jnp
from jax import lax
from jax.sharding import PartitionSpec as P

ITERS = 2


def split_points(bloch_const, local_points, chosen):
    components = bloch_const.shape[0]
    reshaped = bloch_const.reshape(components, local_points, -1, components)
    return jnp.transpose(reshaped.reshape(components, local_points, chosen * components), (1, 0, 2))


def coupling_fold(carried, shard_in, first_row, const_blocks, delta_local, inv_count):
    lead_size = shard_in.shape[0]
    piece_len = shard_in.shape[1]
    components = shard_in.shape[2]
    flat_rows = shard_in.reshape(lead_size * piece_len, components)

    def per_point(const_block):
        amplitude = jnp.dot(flat_rows, const_block, preferred_element_type=jnp.float32)
        amplitude = amplitude.reshape(lead_size * piece_len, -1, components)
        return jnp.sum(amplitude * amplitude, axis=2)

    squared = lax.map(per_point, const_blocks)
    squared = jnp.transpose(squared, (1, 0, 2)).reshape(lead_size, piece_len, -1)
    weight_block = delta_local.astype(jnp.float32)
    return squared * weight_block * inv_count


def branch_total(partial_sum):
    own_count = partial_sum.shape[1] // lax.axis_size("br")
    summed = lax.psum(partial_sum, "br")
    return lax.dynamic_slice_in_dim(summed, lax.axis_index("br") * own_count, own_count, 1)


def full_deviation(deviation):
    return lax.all_gather(deviation, "pb", axis=0, tiled=True)


def on_device(bloch_const, polarization, delta_weight, partner, velocity, capacity):
    local_points = velocity.shape[0]
    own_count = velocity.shape[1]
    all_branches = own_count * lax.axis_size("br")
    total_points = polarization.shape[1] * lax.axis_size("pb")
    inv_count = 1.0 / (total_points * all_branches)
    const_blocks = split_points(bloch_const, local_points, all_branches)
    zero_start = jnp.zeros((own_count, total_points, local_points * all_branches), jnp.float32)
    folder = partial(
        coupling_fold, const_blocks=const_blocks, delta_local=delta_weight, inv_count=inv_count
    )
    coupling = folder(
        zero_start, lax.all_gather(polarization, "pb", axis=1, tiled=True), jnp.int32(0)
    )
    coupling = coupling.reshape(own_count, total_points, local_points, all_branches)
    rate_total = branch_total(jnp.sum(coupling, axis=(0, 1)))
    deviation = velocity / rate_total
    heat_weight = capacity * velocity
    kappas = []
    for sweep_index in range(ITERS):
        deviation_all = full_deviation(deviation)
        partner_value = deviation_all[partner]
        combined = jnp.transpose(deviation_all)[:, :, None] + jnp.transpose(
            partner_value, (2, 1, 0)
        )
        spread = jnp.einsum("abqs,abq->qs", coupling, combined, precision=lax.Precision.HIGHEST)
        spread = branch_total(spread)
        deviation = (velocity + 0.5 * spread) / rate_total
        kappa_term = jnp.sum(heat_weight * deviation) * inv_count
        kappas.append(lax.psum(kappa_term, ("pb", "br")))
    kappa = jnp.stack(kappas)
    return (deviation, kappa)


def solution(mesh):
    in_specs = (
        P(None, "pb"),
        P("br", "pb", None),
        P("br", None, "pb"),
        P("pb", None),
        P("pb", "br"),
        P("pb", "br"),
    )
    out_specs = (P("pb", "br"), P())
    return jax.shard_map(
        on_device, mesh=mesh, in_specs=in_specs, out_specs=out_specs, check_vma=False
    )
```

profile of v0, /device:TPU:1, one launch (start us, length us, event | category | flops | bytes accessed | tf_op | source)
XLA Modules:
  0.0 1065.5 jit_solution(7599198885120095185)
XLA Ops:
  3.1 163.8 %all_gather.9 = bf16[9,512,36]{2,1,0:T(8,128)(2,1)S(1)} all-gather(bf16[9,8,36]{2,1,0:T(8,128)(2,1)} %param.9), channel_id=1, replica_groups=mesh['pb'=64,'br'=4] {'pb'}, dimensions={1}, use_global_device_ids=true | all-gather | bytes 336960 | tf_op jit(solution)/shard_map/all_gather | solution.py:55
  166.9 349.9 %while.10 = (s32[]{:T(128)}, f32[8,4608,36]{1,2,0:T(8,128)}, bf16[8,36,1296]{2,1,0:T(8,128)(2,1)S(1)}, bf16[4608,36]{1,0:T(8,128)(2,1)S(1)}, s32[]{:T(128)}, /*index=5*/f32[]{:T(128)}) while((s32[]{:T(128)}, f32[8,4608,36]{1,2,0:T(8,128)}, bf16[8,36,1296]{2,1,0:T(8,128)(2,1)S(1)}, bf16[4608,36]{1,0:T(8,128)(2,1)S(1)}, s32[]{:T(128)}, ...), condition=%wide.region_2.3_spmd, body=%wide.region_0.2_spmd.sunk | while | flops 441759744 | bytes 98908744 | solution.py:27
  176.6 23.2 %mul.74 = f32[4608,36,36]{0,2,1:T(8,128)} reshape(f32[4608,1296]{0,1:T(8,128)} %fusion.18) | data formatting | bytes 47775744 | tf_op jit(solution)/shard_map/while/body/eval_jaxpr/mul | solution.py:25
  199.8 9.9 reduce_sum.46
  220.3 23.2 %mul.74 = f32[4608,36,36]{0,2,1:T(8,128)} reshape(f32[4608,1296]{0,1:T(8,128)} %fusion.18) | data formatting | bytes 47775744 | tf_op jit(solution)/shard_map/while/body/eval_jaxpr/mul | solution.py:25
  243.5 9.9 reduce_sum.46
  254.4 9.7 fusion.18
  264.1 23.2 %mul.74 = f32[4608,36,36]{0,2,1:T(8,128)} reshape(f32[4608,1296]{0,1:T(8,128)} %fusion.18) | data formatting | bytes 47775744 | tf_op jit(solution)/shard_map/while/body/eval_jaxpr/mul | solution.py:25
  287.3 9.9 reduce_sum.46
  298.1 9.7 fusion.18
  307.9 23.2 %mul.74 = f32[4608,36,36]{0,2,1:T(8,128)} reshape(f32[4608,1296]{0,1:T(8,128)} %fusion.18) | data formatting | bytes 47775744 | tf_op jit(solution)/shard_map/while/body/eval_jaxpr/mul | solution.py:25
  331.0 9.9 reduce_sum.46
  351.6 23.2 %mul.74 = f32[4608,36,36]{0,2,1:T(8,128)} reshape(f32[4608,1296]{0,1:T(8,128)} %fusion.18) | data formatting | bytes 47775744 | tf_op jit(solution)/shard_map/while/body/eval_jaxpr/mul | solution.py:25
  374.7 9.9 reduce_sum.46
  385.6 9.7 fusion.18
  395.3 23.2 %mul.74 = f32[4608,36,36]{0,2,1:T(8,128)} reshape(f32[4608,1296]{0,1:T(8,128)} %fusion.18) | data formatting | bytes 47775744 | tf_op jit(solution)/shard_map/while/body/eval_jaxpr/mul | solution.py:25
  418.5 9.9 reduce_sum.46
  439.1 23.2 %mul.74 = f32[4608,36,36]{0,2,1:T(8,128)} reshape(f32[4608,1296]{0,1:T(8,128)} %fusion.18) | data formatting | bytes 47775744 | tf_op jit(solution)/shard_map/while/body/eval_jaxpr/mul | solution.py:25
  462.2 9.9 reduce_sum.46
  482.8 23.2 %mul.74 = f32[4608,36,36]{0,2,1:T(8,128)} reshape(f32[4608,1296]{0,1:T(8,128)} %fusion.18) | data formatting | bytes 47775744 | tf_op jit(solution)/shard_map/while/body/eval_jaxpr/mul | solution.py:25
  506.0 9.9 reduce_sum.46
  524.1 9.9 fusion.9
  534.0 33.8 %psum.35 = f32[8,36]{1,0:T(8,128)S(1)} all-reduce(f32[8,36]{1,0:T(8,128)S(1)} %reduce_sum.39), channel_id=1, replica_groups=mesh['pb'=64,'br'=4] {'br'}, use_global_device_ids=true, to_apply=%region_4.5 | all-reduce | flops 288 | bytes 2304 | tf_op jit(solution)/shard_map/psum | solution.py:35
  567.9 147.9 %all_gather.10 = f32[512,9]{1,0:T(8,128)S(1)} all-gather(f32[8,9]{1,0:T(8,128)S(1)} %dynamic-slice_divide_fusion), channel_id=1, replica_groups=mesh['pb'=64,'br'=4] {'pb'}, dimensions={0}, use_global_device_ids=true | all-gather | bytes 18720 | tf_op jit(solution)/shard_map/all_gather | solution.py:40
  715.9 14.1 %gather_fusion = f32[4096,9]{1,0:T(8,128)} fusion(f32[512,9]{1,0:T(8,128)S(1)} %all_gather.10, s32[4096]{0:T(1024)S(1)} %broadcast_clamp_fusion), kind=kCustom, calls=%fused_computation | custom fusion | bytes 311296 | tf_op jit(solution)/shard_map/gather | solution.py:64
  732.5 11.1 %fusion.6 = f32[8,1,36,1]{2,1,0,3:T(1,128)S(1)} fusion(f32[9,512,8,1]{1,3,2,0:T(1,128)S(1)} %copy.15, f32[9,512,8,36]{1,0,3,2:T(8,128)} %bitcast.51), kind=kOutput, calls=%fused_computation.11 | convolution fusion | flops 15925248 | bytes 5457024 | tf_op jit(solution)/shard_map/abqs,abq->qs/dot_general | solution.py:68
  743.6 33.2 %psum.36 = f32[8,36]{1,0:T(8,128)S(1)} all-reduce(f32[8,36]{1,0:T(8,128)S(1)} %bitcast.60), channel_id=1, replica_groups=mesh['pb'=64,'br'=4] {'br'}, use_global_device_ids=true, to_apply=%region_5.6 | all-reduce | flops 288 | bytes 2304 | tf_op jit(solution)/shard_map/psum | solution.py:35
  776.9 149.5 %all_gather.11 = f32[512,9]{1,0:T(8,128)S(1)} all-gather(f32[8,9]{1,0:T(8,128)S(1)} %add_divide_fusion.1), channel_id=1, replica_groups=mesh['pb'=64,'br'=4] {'pb'}, dimensions={0}, use_global_device_ids=true | all-gather | bytes 18720 | tf_op jit(solution)/shard_map/all_gather | solution.py:40
  926.4 14.1 %gather_fusion.1 = f32[4096,9]{1,0:T(8,128)} fusion(f32[512,9]{1,0:T(8,128)S(1)} %all_gather.11, s32[4096]{0:T(1024)S(1)} %broadcast_clamp_fusion), kind=kCustom, calls=%fused_computation.1 | custom fusion | bytes 311296 | tf_op jit(solution)/shard_map/gather | solution.py:64
  943.0 11.1 %fusion.4 = f32[8,1,36,1]{2,1,0,3:T(1,128)S(1)} fusion(f32[9,512,8,1]{1,3,2,0:T(1,128)S(1)} %copy.17, f32[9,512,8,36]{1,0,3,2:T(8,128)} %bitcast.52), kind=kOutput, calls=%fused_computation.9 | convolution fusion | flops 15925248 | bytes 5457024 | tf_op jit(solution)/shard_map/abqs,abq->qs/dot_general | solution.py:68
  954.2 33.4 %psum.37 = f32[8,36]{1,0:T(8,128)S(1)} all-reduce(f32[8,36]{1,0:T(8,128)S(1)} %bitcast.59), channel_id=1, replica_groups=mesh['pb'=64,'br'=4] {'br'}, use_global_device_ids=true, to_apply=%region_6.7 | all-reduce | flops 288 | bytes 2304 | tf_op jit(solution)/shard_map/psum | solution.py:35
  990.1 73.6 %all-reduce = (f32[1]{0:T(128)}, f32[1]{0:T(128)}) all-reduce(f32[1]{0:T(128)} %bitcast.20, f32[1]{0:T(128)} %bitcast.19), channel_id=1, replica_groups=mesh['pb'=64,'br'=4] {'pb','br'}, use_global_device_ids=true, to_apply=%region_10.11 | all-reduce | flops 2 | bytes 16 | tf_op jit(solution)/shard_map/psum | solution.py:72
  (37 shorter events, 74.1 us)
Async XLA Ops:
  516.8 7.2 copy-start
  524.1 43.8 %copy-start.1 = (f32[8,9]{1,0:T(8,128)S(1)}, f32[8,9]{1,0:T(8,128)}, u32[]{:S(2)}) copy-start(f32[8,9]{1,0:T(8,128)} %param.12) | copy-start | bytes 868
  524.1 191.8 %copy-start.2 = (s32[8,512]{1,0:T(8,128)S(1)}, s32[8,512]{1,0:T(8,128)}, u32[]{:S(2)}) copy-start(s32[8,512]{1,0:T(8,128)} %param.11) | copy-start | bytes 49156
  940.4 47.1 %copy-start.3 = (f32[8,9]{1,0:T(8,128)S(1)}, f32[8,9]{1,0:T(8,128)}, u32[]{:S(2)}) copy-start(f32[8,9]{1,0:T(8,128)} %param.13) | copy-start | bytes 868
where the time goes:
time: 1070 us
  blocking collectives  635 us (59%)
  local copies, waits for them, and re-layouts  232 us (22%)
  matrix products  99.9 us (9%)
  other arithmetic  96.2 us (9%)
    all_gather x2, blocking collectives, full_deviation(): return lax.all_gather(deviation, 'pb', axis=0, tiled=True)  297 us
    mul x8, local copies, waits for them, and re-layouts, per_point(): return jnp.sum(amplitude * amplitude, axis=2)  185 us
    all_gather x1, blocking collectives, on_device(): lax.all_gather(polarization, 'pb', axis=1, tiled=True)  164 us
    psum x3, blocking collectives, branch_total(): summed = lax.psum(partial_sum, 'br')  100 us
    reduce_sum x8, other arithmetic, per_point(): return jnp.sum(amplitude * amplitude, axis=2)  79.6 us
    dot_general x8, matrix products, per_point(): jnp.dot(flat_rows, const_block, preferred_element_type=jnp.float32)  77.6 us
    psum x1, blocking collectives, on_device(): kappas.append(lax.psum(kappa_term, ('pb', 'br')))  73.6 us
    gather x2, local copies, waits for them, and re-layouts, on_device(): partner_value = deviation_all[partner]  28.1 us

commit v1 on v0

--- a/solution.py
+++ b/solution.py
@@ -52,7 +52,14 @@
         coupling_fold, const_blocks=const_blocks, delta_local=delta_weight, inv_count=inv_count
     )
     coupling = folder(
-        zero_start, lax.all_gather(polarization, "pb", axis=1, tiled=True), jnp.int32(0)
+        zero_start,
+        jnp.concatenate(
+            jax.lax.all_to_all(
+                jnp.stack([polarization for _ in range(jax.lax.axis_size("pb"))]), "pb", 0, 0
+            ),
+            axis=1,
+        ),
+        jnp.int32(0),
     )
     coupling = coupling.reshape(own_count, total_points, local_points, all_branches)
     rate_total = branch_total(jnp.sum(coupling, axis=(0, 1)))

time: 1070 us -> 914 us (0.85)
  blocking collectives: 635 us -> 448 us
  starting transfers between devices: 0 us -> 15.1 us
    all_gather x1 -> x0, blocking collectives: 164 us -> none  [on_device(): lax.all_gather(polarization, 'pb', axis=1, tiled=True)]
    psum x3, blocking collectives: 100 us -> 74.7 us  [branch_total(): summed = lax.psum(partial_sum, 'br')]
    all_to_all x0 -> x1, starting transfers between devices: none -> 15.1 us  [on_device(): jax.lax.all_to_all(jnp.stack([polarization for _ in range(jax.lax.axis_si...]
  transfers between devices with their start and end apart: 0 -> 1, of which waited for: 0 -> 1; matrix products, arithmetic and copies ran while one was open for 0% -> 0% of each run, Pallas kernels for 0% -> 0%
where the time goes in v1:
time: 914 us; the launch traced here: 909 us
  blocking collectives  448 us (49%)
  local copies, waits for them, and re-layouts  237 us (26%)
  matrix products  99.9 us (11%)
  other arithmetic  96.8 us (11%)
  starting transfers between devices  15.1 us (2%)
  waiting for transfers between devices  10 us (1%)
    all_gather x2, blocking collectives, full_deviation(): return lax.all_gather(deviation, 'pb', axis=0, tiled=True)  299 us
    mul x8, local copies, waits for them, and re-layouts, per_point(): return jnp.sum(amplitude * amplitude, axis=2)  185 us
    reduce_sum x8, other arithmetic, per_point(): return jnp.sum(amplitude * amplitude, axis=2)  79.6 us
    dot_general x8, matrix products, per_point(): jnp.dot(flat_rows, const_block, preferred_element_type=jnp.float32)  77.6 us
    psum x3, blocking collectives, branch_total(): summed = lax.psum(partial_sum, 'br')  74.7 us
    psum x1, blocking collectives, on_device(): kappas.append(lax.psum(kappa_term, ('pb', 'br')))  74.3 us
    gather x2, local copies, waits for them, and re-layouts, on_device(): partner_value = deviation_all[partner]  28.1 us
    dot_general x2, matrix products, on_device(): jnp.einsum('abqs,abq->qs', coupling, combined, precision=lax.Precision.HI...  22.3 us
  transfers between devices with their start and end apart: 1, of which 1 were waited for; matrix products, arithmetic and copies ran while one was open for 0% of the time, Pallas kernels for 0%

profile of v1, /device:TPU:1, one launch (start us, length us, event | category | flops | bytes accessed | tf_op | source)
XLA Modules:
  0.0 908.6 jit_solution(9036719811943421128)
XLA Ops:
  4.0 15.1 %all-to-all-start = ((bf16[64,2,1296]{2,1,0:T(2,128)(2,1)}), bf16[64,2,1296]{2,1,0:T(2,128)(2,1)S(1)}, u32[]{:S(2)}, u32[]{:S(2)}) async-start(bf16[64,2,1296]{2,1,0:T(2,128)(2,1)} %reshape.47), calls=%async_computation | async-start | bytes 720896 | tf_op jit(solution)/shard_map/all_to_all | solution.py:57
  22.2 10.0 %all-to-all-done = bf16[64,2,1296]{2,1,0:T(2,128)(2,1)S(1)} async-done(((bf16[64,2,1296]{2,1,0:T(2,128)(2,1)}), bf16[64,2,1296]{2,1,0:T(2,128)(2,1)S(1)}, u32[]{:S(2)}, u32[]{:S(2)}) %all-to-all-start) | async-done | bytes 331808 | tf_op jit(solution)/shard_map/all_to_all | solution.py:57
  33.6 350.0 %while.10 = (s32[]{:T(128)}, f32[8,4608,36]{1,2,0:T(8,128)}, bf16[8,36,1296]{2,1,0:T(8,128)(2,1)S(1)}, bf16[4608,36]{1,0:T(8,128)(2,1)S(1)}, s32[]{:T(128)}, /*index=5*/f32[]{:T(128)}) while((s32[]{:T(128)}, f32[8,4608,36]{1,2,0:T(8,128)}, bf16[8,36,1296]{2,1,0:T(8,128)(2,1)S(1)}, bf16[4608,36]{1,0:T(8,128)(2,1)S(1)}, s32[]{:T(128)}, ...), condition=%wide.region_2.3_spmd, body=%wide.region_0.2_spmd.sunk | while | flops 441759744 | bytes 98908744 | solution.py:27
  33.6 9.7 %fusion.18 = f32[4608,1296]{0,1:T(8,128)} fusion(bf16[4608,36]{1,0:T(8,128)(2,1)S(1)} %get-tuple-element.92, bf16[8,36,1296]{2,1,0:T(8,128)(2,1)S(1)} %get-tuple-element.91, s32[]{:T(128)} %get-tuple-element.83), kind=kOutput, calls=%fused_computation.3.clone.1 | convolution fusion | flops 435953664 | bytes 25180164 | tf_op jit(solution)/shard_map/while/body/eval_jaxpr/dot_general | solution.py:23
  43.4 23.2 %mul.74 = f32[4608,36,36]{0,2,1:T(8,128)} reshape(f32[4608,1296]{0,1:T(8,128)} %fusion.18) | data formatting | bytes 47775744 | tf_op jit(solution)/shard_map/while/body/eval_jaxpr/mul | solution.py:25
  66.5 9.9 %reduce_sum.46 = f32[4608,36]{0,1:T(8,128)S(1)} reduce(f32[4608,36,36]{0,2,1:T(8,128)} %mul.74, f32[]{:T(128)} %constant.7.clone.1..sunk), dimensions={2}, to_apply=%region_1.1 | reduce | flops 5806080 | bytes 24551428 | tf_op jit(solution)/shard_map/while/body/eval_jaxpr/reduce_sum | solution.py:25
  77.4 9.7 %fusion.18 = f32[4608,1296]{0,1:T(8,128)} fusion(bf16[4608,36]{1,0:T(8,128)(2,1)S(1)} %get-tuple-element.92, bf16[8,36,1296]{2,1,0:T(8,128)(2,1)S(1)} %get-tuple-element.91, s32[]{:T(128)} %get-tuple-element.83), kind=kOutput, calls=%fused_computation.3.clone.1 | convolution fusion | flops 435953664 | bytes 25180164 | tf_op jit(solution)/shard_map/while/body/eval_jaxpr/dot_general | solution.py:23
  87.1 23.2 %mul.74 = f32[4608,36,36]{0,2,1:T(8,128)} reshape(f32[4608,1296]{0,1:T(8,128)} %fusion.18) | data formatting | bytes 47775744 | tf_op jit(solution)/shard_map/while/body/eval_jaxpr/mul | solution.py:25
  110.2 9.9 %reduce_sum.46 = f32[4608,36]{0,1:T(8,128)S(1)} reduce(f32[4608,36,36]{0,2,1:T(8,128)} %mul.74, f32[]{:T(128)} %constant.7.clone.1..sunk), dimensions={2}, to_apply=%region_1.1 | reduce | flops 5806080 | bytes 24551428 | tf_op jit(solution)/shard_map/while/body/eval_jaxpr/reduce_sum | solution.py:25
  121.1 9.7 %fusion.18 = f32[4608,1296]{0,1:T(8,128)} fusion(bf16[4608,36]{1,0:T(8,128)(2,1)S(1)} %get-tuple-element.92, bf16[8,36,1296]{2,1,0:T(8,128)(2,1)S(1)} %get-tuple-element.91, s32[]{:T(128)} %get-tuple-element.83), kind=kOutput, calls=%fused_computation.3.clone.1 | convolution fusion | flops 435953664 | bytes 25180164 | tf_op jit(solution)/shard_map/while/body/eval_jaxpr/dot_general | solution.py:23
  130.8 23.2 %mul.74 = f32[4608,36,36]{0,2,1:T(8,128)} reshape(f32[4608,1296]{0,1:T(8,128)} %fusion.18) | data formatting | bytes 47775744 | tf_op jit(solution)/shard_map/while/body/eval_jaxpr/mul | solution.py:25
  154.0 9.9 %reduce_sum.46 = f32[4608,36]{0,1:T(8,128)S(1)} reduce(f32[4608,36,36]{0,2,1:T(8,128)} %mul.74, f32[]{:T(128)} %constant.7.clone.1..sunk), dimensions={2}, to_apply=%region_1.1 | reduce | flops 5806080 | bytes 24551428 | tf_op jit(solution)/shard_map/while/body/eval_jaxpr/reduce_sum | solution.py:25
  174.6 23.2 %mul.74 = f32[4608,36,36]{0,2,1:T(8,128)} reshape(f32[4608,1296]{0,1:T(8,128)} %fusion.18) | data formatting | bytes 47775744 | tf_op jit(solution)/shard_map/while/body/eval_jaxpr/mul | solution.py:25
  197.7 9.9 %reduce_sum.46 = f32[4608,36]{0,1:T(8,128)S(1)} reduce(f32[4608,36,36]{0,2,1:T(8,128)} %mul.74, f32[]{:T(128)} %constant.7.clone.1..sunk), dimensions={2}, to_apply=%region_1.1 | reduce | flops 5806080 | bytes 24551428 | tf_op jit(solution)/shard_map/while/body/eval_jaxpr/reduce_sum | solution.py:25
  218.3 23.2 %mul.74 = f32[4608,36,36]{0,2,1:T(8,128)} reshape(f32[4608,1296]{0,1:T(8,128)} %fusion.18) | data formatting | bytes 47775744 | tf_op jit(solution)/shard_map/while/body/eval_jaxpr/mul | solution.py:25
  241.5 9.9 %reduce_sum.46 = f32[4608,36]{0,1:T(8,128)S(1)} reduce(f32[4608,36,36]{0,2,1:T(8,128)} %mul.74, f32[]{:T(128)} %constant.7.clone.1..sunk), dimensions={2}, to_apply=%region_1.1 | reduce | flops 5806080 | bytes 24551428 | tf_op jit(solution)/shard_map/while/body/eval_jaxpr/reduce_sum | solution.py:25
  262.1 23.2 %mul.74 = f32[4608,36,36]{0,2,1:T(8,128)} reshape(f32[4608,1296]{0,1:T(8,128)} %fusion.18) | data formatting | bytes 47775744 | tf_op jit(solution)/shard_map/while/body/eval_jaxpr/mul | solution.py:25
  285.2 9.9 %reduce_sum.46 = f32[4608,36]{0,1:T(8,128)S(1)} reduce(f32[4608,36,36]{0,2,1:T(8,128)} %mul.74, f32[]{:T(128)} %constant.7.clone.1..sunk), dimensions={2}, to_apply=%region_1.1 | reduce | flops 5806080 | bytes 24551428 | tf_op jit(solution)/shard_map/while/body/eval_jaxpr/reduce_sum | solution.py:25
  305.8 23.2 %mul.74 = f32[4608,36,36]{0,2,1:T(8,128)} reshape(f32[4608,1296]{0,1:T(8,128)} %fusion.18) | data formatting | bytes 47775744 | tf_op jit(solution)/shard_map/while/body/eval_jaxpr/mul | solution.py:25
  329.0 9.9 %reduce_sum.46 = f32[4608,36]{0,1:T(8,128)S(1)} reduce(f32[4608,36,36]{0,2,1:T(8,128)} %mul.74, f32[]{:T(128)} %constant.7.clone.1..sunk), dimensions={2}, to_apply=%region_1.1 | reduce | flops 5806080 | bytes 24551428 | tf_op jit(solution)/shard_map/while/body/eval_jaxpr/reduce_sum | solution.py:25
  349.5 23.2 %mul.74 = f32[4608,36,36]{0,2,1:T(8,128)} reshape(f32[4608,1296]{0,1:T(8,128)} %fusion.18) | data formatting | bytes 47775744 | tf_op jit(solution)/shard_map/while/body/eval_jaxpr/mul | solution.py:25
  372.7 9.9 %reduce_sum.46 = f32[4608,36]{0,1:T(8,128)S(1)} reduce(f32[4608,36,36]{0,2,1:T(8,128)} %mul.74, f32[]{:T(128)} %constant.7.clone.1..sunk), dimensions={2}, to_apply=%region_1.1 | reduce | flops 5806080 | bytes 24551428 | tf_op jit(solution)/shard_map/while/body/eval_jaxpr/reduce_sum | solution.py:25
  390.8 9.9 %fusion.9 = (f32[288]{0:T(512)S(1)}, f32[9,512,288]{1,0,2:T(8,128)}) fusion(f32[9,512,288]{1,0,2:T(8,128)} %reshape.21, bf16[9,512,288]{1,2,0:T(8,128)(2,1)S(1)} %copy-done), kind=kLoop, calls=%fused_computation.24 | loop fusion | flops 5308128 | bytes 13272192 | tf_op jit(solution)/shard_map/reduce_sum | solution.py:65
  409.1 151.1 %all_gather.6 = f32[512,9]{1,0:T(8,128)S(1)} all-gather(f32[8,9]{1,0:T(8,128)S(1)} %dynamic-slice_divide_fusion), channel_id=1, replica_groups=mesh['pb'=64,'br'=4] {'pb'}, dimensions={0}, use_global_device_ids=true | all-gather | bytes 18720 | tf_op jit(solution)/shard_map/all_gather | solution.py:40
  560.2 14.1 %gather_fusion = f32[4096,9]{1,0:T(8,128)} fusion(f32[512,9]{1,0:T(8,128)S(1)} %all_gather.6, s32[4096]{0:T(1024)S(1)} %copy-done.1), kind=kCustom, calls=%fused_computation | custom fusion | bytes 311296 | tf_op jit(solution)/shard_map/gather | solution.py:71
  576.8 11.1 %fusion.6 = f32[8,1,36,1]{2,1,0,3:T(1,128)S(1)} fusion(f32[9,512,8,1]{1,3,2,0:T(1,128)S(1)} %copy.19, f32[9,512,8,36]{1,0,3,2:T(8,128)} %bitcast.52), kind=kOutput, calls=%fused_computation.11 | convolution fusion | flops 15925248 | bytes 5457024 | tf_op jit(solution)/shard_map/abqs,abq->qs/dot_general | solution.py:75
  588.0 33.3 %psum.36 = f32[8,36]{1,0:T(8,128)S(1)} all-reduce(f32[8,36]{1,0:T(8,128)S(1)} %bitcast.62), channel_id=1, replica_groups=mesh['pb'=64,'br'=4] {'br'}, use_global_device_ids=true, to_apply=%region_5.6 | all-reduce | flops 288 | bytes 2304 | tf_op jit(solution)/shard_map/psum | solution.py:35
  621.4 147.7 %all_gather.7 = f32[512,9]{1,0:T(8,128)S(1)} all-gather(f32[8,9]{1,0:T(8,128)S(1)} %add_divide_fusion.1), channel_id=1, replica_groups=mesh['pb'=64,'br'=4] {'pb'}, dimensions={0}, use_global_device_ids=true | all-gather | bytes 18720 | tf_op jit(solution)/shard_map/all_gather | solution.py:40
  769.1 14.1 %gather_fusion.1 = f32[4096,9]{1,0:T(8,128)} fusion(f32[512,9]{1,0:T(8,128)S(1)} %all_gather.7, s32[4096]{0:T(1024)S(1)} %copy-done.1), kind=kCustom, calls=%fused_computation.1 | custom fusion | bytes 311296 | tf_op jit(solution)/shard_map/gather | solution.py:71
  785.7 11.1 %fusion.4 = f32[8,1,36,1]{2,1,0,3:T(1,128)S(1)} fusion(f32[9,512,8,1]{1,3,2,0:T(1,128)S(1)} %copy.21, f32[9,512,8,36]{1,0,3,2:T(8,128)} %bitcast.53), kind=kOutput, calls=%fused_computation.9 | convolution fusion | flops 15925248 | bytes 5457024 | tf_op jit(solution)/shard_map/abqs,abq->qs/dot_general | solution.py:75
  796.9 33.2 %psum.37 = f32[8,36]{1,0:T(8,128)S(1)} all-reduce(f32[8,36]{1,0:T(8,128)S(1)} %bitcast.61), channel_id=1, replica_groups=mesh['pb'=64,'br'=4] {'br'}, use_global_device_ids=true, to_apply=%region_6.7 | all-reduce | flops 288 | bytes 2304 | tf_op jit(solution)/shard_map/psum | solution.py:35
  832.5 74.3 %all-reduce = (f32[1]{0:T(128)}, f32[1]{0:T(128)}) all-reduce(f32[1]{0:T(128)} %bitcast.21, f32[1]{0:T(128)} %bitcast.20), channel_id=1, replica_groups=mesh['pb'=64,'br'=4] {'pb','br'}, use_global_device_ids=true, to_apply=%region_10.11 | all-reduce | flops 2 | bytes 16 | tf_op jit(solution)/shard_map/psum | solution.py:79
  (44 shorter events, 87.6 us)
Async XLA Ops:
  0.6 20.9 %copy-start.3 = (s32[8,512]{1,0:T(8,128)S(1)}, s32[8,512]{1,0:T(8,128)}, u32[]{:S(2)}) copy-start(s32[8,512]{1,0:T(8,128)} %param.11) | copy-start | bytes 49156
  4.0 28.2 %all-to-all-start = ((bf16[64,2,1296]{2,1,0:T(2,128)(2,1)}), bf16[64,2,1296]{2,1,0:T(2,128)(2,1)S(1)}, u32[]{:S(2)}, u32[]{:S(2)}) async-start(bf16[64,2,1296]{2,1,0:T(2,128)(2,1)} %reshape.47), calls=%async_computation | async-start | bytes 720896 | tf_op jit(solution)/shard_map/all_to_all | solution.py:57
  383.6 7.2 copy-start
  390.8 18.2 %copy-start.2 = (f32[8,9]{1,0:T(8,128)S(1)}, f32[8,9]{1,0:T(8,128)}, u32[]{:S(2)}) copy-start(f32[8,9]{1,0:T(8,128)} %param.12) | copy-start | bytes 868
  390.8 169.4 %copy-start.1 = (s32[4096]{0:T(1024)S(1)}, s32[4096]{0:T(1024)}, u32[]{:S(2)}) copy-start(s32[4096]{0:T(1024)} %broadcast_clamp_fusion) | copy-start | bytes 49156
  783.1 46.9 %copy-start.4 = (f32[8,9]{1,0:T(8,128)S(1)}, f32[8,9]{1,0:T(8,128)}, u32[]{:S(2)}) copy-start(f32[8,9]{1,0:T(8,128)} %param.13) | copy-start | bytes 868
